TPU v7x, 32 devices: a whole 2x2x4 slice. The times are simulated.
32 devices in a mesh: sect: 2 (over x), seq: 4 (over y, core), dp: 4 (over z).
Axes of the slice: x: 2, y: 2, z: 4, core: 2. Of those that a mesh axis runs over, the one named last changes fastest.
Arguments:
- query_tiles: bfloat16 [4, 8, 128, 2048], P('dp', None, 'sect', 'seq'), may hold values from -6 to 6
- key_tiles: bfloat16 [4, 8, 128, 2048], P('dp', None, 'sect', 'seq'), may hold values from -6 to 6
- value_tiles: bfloat16 [4, 8, 128, 2048], P('dp', None, 'sect', 'seq'), may hold values from -6 to 6
- text_keys: bfloat16 [8, 256, 2048], P(('sect', 'dp'), 'seq'), may hold values from -6 to 6
- text_values: bfloat16 [8, 256, 2048], P(('sect', 'dp'), 'seq'), may hold values from -6 to 6
- text_lengths: int32 [8], P(('sect', 'dp')), may hold values from 32 to 256, as said below
- tile_place: int32 [4], replicated, may hold values from 0 to 3, each once
Outputs:
- attended: bfloat16 [8, 512, 2048], P(('sect', 'dp'), 'seq')
Inputs may be any that keep to these rules, and one draw needn't show every extreme that they name: `tile_place`: each spatial position is held by exactly one tile slot. `text_lengths`: the live text tokens of a clip are its first rows; some clip fills all 256 slots.
All inputs are finite; a program needn't handle non-finite values.
Results may differ from a plain program's by a relative error of at most 0.0031.
Values may be sent and summed in bfloat16 or wider, within the bound.
A program may use at most 64 MiB of HBM per device.

v0:
```python
import math

import jax
import jax.numpy as jnp
from jax import lax
from jax.sharding import PartitionSpec as P

HD = 128


def attend(queries_flat, keys_video, values_video, keys_text, values_text, length):
    query_rows, head_width = queries_flat.shape
    head_count = head_width // HD
    score_scale = 1.0 / math.sqrt(HD)
    keys_video = keys_video.reshape(-1, head_count, HD)
    values_video = values_video.reshape(-1, head_count, HD)
    keys_text = keys_text.reshape(-1, head_count, HD)
    values_text = values_text.reshape(-1, head_count, HD)
    live_mask = jnp.arange(keys_text.shape[0], dtype=jnp.int32) < length
    block_rows = math.gcd(query_rows, 512)

    def one_block(query_block):
        score_video = (
            jnp.einsum("qhd,khd->hqk", query_block, keys_video, preferred_element_type=jnp.float32)
            * score_scale
        )
        score_text = (
            jnp.einsum("qhd,khd->hqk", query_block, keys_text, preferred_element_type=jnp.float32)
            * score_scale
        )
        score_text = jnp.where(live_mask[None, None, :], score_text, -jnp.inf)
        row_max = jnp.maximum(jnp.max(score_video, axis=-1), jnp.max(score_text, axis=-1))[
            ..., None
        ]
        expo_video = jnp.exp(score_video - row_max)
        expo_text = jnp.exp(score_text - row_max)
        denominators = jnp.sum(expo_video, axis=-1) + jnp.sum(expo_text, axis=-1)
        mixed = jnp.einsum(
            "hqk,khd->qhd",
            expo_video.astype(jnp.bfloat16),
            values_video,
            preferred_element_type=jnp.float32,
        )
        mixed = mixed + jnp.einsum(
            "hqk,khd->qhd",
            expo_text.astype(jnp.bfloat16),
            values_text,
            preferred_element_type=jnp.float32,
        )
        return (mixed / jnp.transpose(denominators)[:, :, None]).astype(jnp.bfloat16)

    blocks = queries_flat.reshape(query_rows // block_rows, block_rows, head_count, HD)
    return lax.map(one_block, blocks).reshape(query_rows, head_width)


def shards(query_tiles, key_tiles, value_tiles, text_keys, text_values, text_lengths, tile_place):
    tile_count = lax.axis_size("dp")
    sect_count = lax.axis_size("sect")
    part_rows = query_tiles.shape[2]
    head_width = query_tiles.shape[3]
    tile_seq = part_rows * sect_count

    def regroup(piece):
        return piece.reshape(1, sect_count, tile_count, part_rows, head_width)

    relayed = (
        lax.all_to_all(
            lax.all_to_all(regroup(query_tiles), "sect", split_axis=1, concat_axis=3, tiled=True),
            "dp",
            split_axis=2,
            concat_axis=0,
            tiled=True,
        ),
        lax.all_to_all(
            lax.all_to_all(regroup(key_tiles), "sect", split_axis=1, concat_axis=3, tiled=True),
            "dp",
            split_axis=2,
            concat_axis=0,
            tiled=True,
        ),
        lax.all_to_all(
            lax.all_to_all(regroup(value_tiles), "sect", split_axis=1, concat_axis=3, tiled=True),
            "dp",
            split_axis=2,
            concat_axis=0,
            tiled=True,
        ),
    )
    spatial_order = jnp.argsort(tile_place)
    seq_count = lax.axis_size("seq")
    tile_rows = tile_seq // seq_count

    def arrange(piece):
        grid = piece.reshape(tile_count, seq_count, tile_rows, head_width)
        placed = jnp.take(grid, spatial_order, axis=0)
        placed = jnp.transpose(placed, (1, 0, 2, 3))
        return placed.reshape(seq_count * tile_count * tile_rows, head_width)

    video_queries = arrange(relayed[0])
    video_keys = arrange(relayed[1])
    video_values = arrange(relayed[2])
    keys_text, values_text = (
        lax.all_to_all(text_keys[0], "seq", split_axis=1, concat_axis=0, tiled=True),
        lax.all_to_all(text_values[0], "seq", split_axis=1, concat_axis=0, tiled=True),
    )
    attended_heads = attend(
        video_queries, video_keys, video_values, keys_text, values_text, text_lengths[0]
    )
    attended = lax.all_to_all(attended_heads, "seq", split_axis=0, concat_axis=1, tiled=True)
    return attended[None]


def solution(mesh):
    in_specs = (
        P("dp", None, "sect", "seq"),
        P("dp", None, "sect", "seq"),
        P("dp", None, "sect", "seq"),
        P(("sect", "dp"), "seq", None),
        P(("sect", "dp"), "seq", None),
        P(("sect", "dp")),
        P(),
    )
    out_specs = P(("sect", "dp"), "seq", None)
    return jax.shard_map(shards, mesh=mesh, in_specs=in_specs, out_specs=out_specs, check_vma=False)
```

profile of v0, /device:TPU:0, one launch (start us, length us, event | category | flops | bytes accessed | tf_op | source)
XLA Modules:
  0.0 116.4 jit_solution(8662692775523040408)
XLA Ops:
  0.0 1.2 %all_to_all.111 = bf16[64,4,512]{2,1,0:T(4,128)(2,1)S(1)} reshape(bf16[1,64,2048]{2,1,0:T(8,128)(2,1)} %param.12) | data formatting | bytes 524288 | tf_op jit(solution)/shard_map/all_to_all | solution.py:103
  1.2 0.7 copy.57
  2.0 4.2 %all-to-all-start.6 = ((bf16[64,4,512]{2,0,1:T(8,128)(2,1)}), bf16[64,4,512]{2,0,1:T(8,128)(2,1)S(1)}, u32[]{:S(2)}, u32[]{:S(2)}) async-start(bf16[64,4,512]{2,0,1:T(8,128)(2,1)} %copy.57), calls=%async_computation.6 | async-start | bytes 524288 | tf_op jit(solution)/shard_map/all_to_all | solution.py:103
  6.2 1.1 all_to_all.114
  7.4 4.8 %all-to-all-done.6 = bf16[64,4,512]{2,0,1:T(8,128)(2,1)S(1)} async-done(((bf16[64,4,512]{2,0,1:T(8,128)(2,1)}), bf16[64,4,512]{2,0,1:T(8,128)(2,1)S(1)}, u32[]{:S(2)}, u32[]{:S(2)}) %all-to-all-start.6) | async-done | bytes 262176 | tf_op jit(solution)/shard_map/all_to_all | solution.py:103
  12.3 8.4 %all_to_all.129 = bf16[64,4,512]{2,0,1:T(8,128)(2,1)S(1)} all-to-all(bf16[64,4,512]{2,0,1:T(8,128)(2,1)S(1)} %copy.62), channel_id=1, replica_groups=mesh['sect'=2,'seq'=4,'dp'=4] {'seq'}, dimensions={1} | all-to-all | bytes 524288 | tf_op jit(solution)/shard_map/all_to_all | solution.py:104
  20.7 10.7 %all_to_all.130 = bf16[1,2,4,64,512]{4,3,2,0,1:T(8,128)(2,1)S(1)} all-to-all(bf16[1,2,4,64,512]{4,3,2,0,1:T(8,128)(2,1)S(1)} %bitcast.72), channel_id=1, replica_groups=mesh['sect'=2,'seq'=4,'dp'=4] {'sect'}, dimensions={1} | all-to-all | bytes 1048576 | tf_op jit(solution)/shard_map/all_to_all | solution.py:68
  31.4 9.1 %all_to_all.131 = bf16[1,2,4,64,512]{4,3,2,0,1:T(8,128)(2,1)S(1)} all-to-all(bf16[1,2,4,64,512]{4,3,2,0,1:T(8,128)(2,1)S(1)} %bitcast.73), channel_id=1, replica_groups=mesh['sect'=2,'seq'=4,'dp'=4] {'sect'}, dimensions={1} | all-to-all | bytes 1048576 | tf_op jit(solution)/shard_map/all_to_all | solution.py:75
  40.5 3.5 %all-to-all-start = ((bf16[1,2,4,64,512]{4,3,2,0,1:T(8,128)(2,1)}), bf16[1,2,4,64,512]{4,3,2,0,1:T(8,128)(2,1)S(1)}, u32[]{:S(2)}, u32[]{:S(2)}) async-start(bf16[1,2,4,64,512]{4,3,2,0,1:T(8,128)(2,1)} %bitcast.1), calls=%async_computation | async-start | bytes 1048576 | tf_op jit(solution)/shard_map/all_to_all | solution.py:82
  44.0 0.8 copy.48
  44.8 5.7 %all-to-all-done = bf16[1,2,4,64,512]{4,3,2,0,1:T(8,128)(2,1)S(1)} async-done(((bf16[1,2,4,64,512]{4,3,2,0,1:T(8,128)(2,1)}), bf16[1,2,4,64,512]{4,3,2,0,1:T(8,128)(2,1)S(1)}, u32[]{:S(2)}, u32[]{:S(2)}) %all-to-all-start) | async-done | bytes 524320 | tf_op jit(solution)/shard_map/all_to_all | solution.py:82
  50.6 5.1 %all-to-all-start.3 = ((bf16[1,1,4,128,512]{4,3,1,0,2:T(8,128)(2,1)}), bf16[1,1,4,128,512]{4,3,1,0,2:T(8,128)(2,1)S(1)}, u32[]{:S(2)}, u32[]{:S(2)}) async-start(bf16[1,1,4,128,512]{4,3,1,0,2:T(8,128)(2,1)} %bitcast.13), calls=%async_computation.3 | async-start | bytes 1048576 | tf_op jit(solution)/shard_map/all_to_all | solution.py:67
  55.7 0.8 copy.52
  56.5 10.1 %all-to-all-done.3 = bf16[1,1,4,128,512]{4,3,1,0,2:T(8,128)(2,1)S(1)} async-done(((bf16[1,1,4,128,512]{4,3,1,0,2:T(8,128)(2,1)}), bf16[1,1,4,128,512]{4,3,1,0,2:T(8,128)(2,1)S(1)}, u32[]{:S(2)}, u32[]{:S(2)}) %all-to-all-start.3) | async-done | bytes 524320 | tf_op jit(solution)/shard_map/all_to_all | solution.py:67
  66.7 3.5 %all-to-all-start.5 = ((bf16[1,1,4,128,512]{4,3,1,0,2:T(8,128)(2,1)}), bf16[1,1,4,128,512]{4,3,1,0,2:T(8,128)(2,1)S(1)}, u32[]{:S(2)}, u32[]{:S(2)}) async-start(bf16[1,1,4,128,512]{4,3,1,0,2:T(8,128)(2,1)} %bitcast.21), calls=%async_computation.5 | async-start | bytes 1048576 | tf_op jit(solution)/shard_map/all_to_all | solution.py:74
  70.2 0.8 copy.44
  71.0 10.7 %all-to-all-done.5 = bf16[1,1,4,128,512]{4,3,1,0,2:T(8,128)(2,1)S(1)} async-done(((bf16[1,1,4,128,512]{4,3,1,0,2:T(8,128)(2,1)}), bf16[1,1,4,128,512]{4,3,1,0,2:T(8,128)(2,1)S(1)}, u32[]{:S(2)}, u32[]{:S(2)}) %all-to-all-start.5) | async-done | bytes 524320 | tf_op jit(solution)/shard_map/all_to_all | solution.py:74
  81.7 3.5 %all-to-all-start.1 = ((bf16[1,1,4,128,512]{4,3,1,0,2:T(8,128)(2,1)}), bf16[1,1,4,128,512]{4,3,1,0,2:T(8,128)(2,1)S(1)}, u32[]{:S(2)}, u32[]{:S(2)}) async-start(bf16[1,1,4,128,512]{4,3,1,0,2:T(8,128)(2,1)} %bitcast.5), calls=%async_computation.1 | async-start | bytes 1048576 | tf_op jit(solution)/shard_map/all_to_all | solution.py:81
  85.9 0.7 sort.17
  86.6 0.8 reshape.75
  87.5 0.6 gather_fusion.1
  88.0 0.6 gather_fusion.2
  88.6 8.7 %all-to-all-done.1 = bf16[1,1,4,128,512]{4,3,1,0,2:T(8,128)(2,1)S(1)} async-done(((bf16[1,1,4,128,512]{4,3,1,0,2:T(8,128)(2,1)}), bf16[1,1,4,128,512]{4,3,1,0,2:T(8,128)(2,1)S(1)}, u32[]{:S(2)}, u32[]{:S(2)}) %all-to-all-start.1) | async-done | bytes 524320 | tf_op jit(solution)/shard_map/all_to_all | solution.py:81
  97.3 0.6 gather_fusion
  98.7 0.7 multiply_reduce_fusion
  99.6 0.5 fusion.6
  100.1 0.5 fusion.7
  100.6 0.7 convolution_bitcast_fusion
  101.3 0.7 fusion
  102.0 0.9 fusion.18
  103.2 12.2 %all_to_all.132 = bf16[4,128,512]{1,2,0:T(8,128)(2,1)S(1)} all-to-all(bf16[4,128,512]{1,2,0:T(8,128)(2,1)S(1)} %copy.66), channel_id=1, replica_groups=mesh['sect'=2,'seq'=4,'dp'=4] {'seq'}, dimensions={0} | all-to-all | bytes 1048576 | tf_op jit(solution)/shard_map/all_to_all | solution.py:109
  115.4 1.0 copy.67
  (26 shorter events, 1.3 us)
Async XLA Ops:
  0.0 20.7 %copy-start = (bf16[1,8,64,512]{3,2,1,0:T(8,128)(2,1)S(1)}, bf16[1,8,64,512]{3,2,1,0:T(8,128)(2,1)}, u32[]{:S(2)}) copy-start(bf16[1,8,64,512]{3,2,1,0:T(8,128)(2,1)} %param.9) | copy-start | bytes 1572868
  0.0 31.4 %copy-start.1 = (bf16[1,8,64,512]{3,2,1,0:T(8,128)(2,1)S(1)}, bf16[1,8,64,512]{3,2,1,0:T(8,128)(2,1)}, u32[]{:S(2)}) copy-start(bf16[1,8,64,512]{3,2,1,0:T(8,128)(2,1)} %param.10) | copy-start | bytes 1572868
  2.0 10.3 %all-to-all-start.6 = ((bf16[64,4,512]{2,0,1:T(8,128)(2,1)}), bf16[64,4,512]{2,0,1:T(8,128)(2,1)S(1)}, u32[]{:S(2)}, u32[]{:S(2)}) async-start(bf16[64,4,512]{2,0,1:T(8,128)(2,1)} %copy.57), calls=%async_computation.6 | async-start | bytes 524288 | tf_op jit(solution)/shard_map/all_to_all | solution.py:103
  40.5 10.1 %all-to-all-start = ((bf16[1,2,4,64,512]{4,3,2,0,1:T(8,128)(2,1)}), bf16[1,2,4,64,512]{4,3,2,0,1:T(8,128)(2,1)S(1)}, u32[]{:S(2)}, u32[]{:S(2)}) async-start(bf16[1,2,4,64,512]{4,3,2,0,1:T(8,128)(2,1)} %bitcast.1), calls=%async_computation | async-start | bytes 1048576 | tf_op jit(solution)/shard_map/all_to_all | solution.py:82
  50.6 16.1 %all-to-all-start.3 = ((bf16[1,1,4,128,512]{4,3,1,0,2:T(8,128)(2,1)}), bf16[1,1,4,128,512]{4,3,1,0,2:T(8,128)(2,1)S(1)}, u32[]{:S(2)}, u32[]{:S(2)}) async-start(bf16[1,1,4,128,512]{4,3,1,0,2:T(8,128)(2,1)} %bitcast.13), calls=%async_computation.3 | async-start | bytes 1048576 | tf_op jit(solution)/shard_map/all_to_all | solution.py:67
  55.7 30.1 %copy-start.3 = (s32[4]{0:T(128)S(1)}, s32[4]{0:T(128)}, u32[]{:S(2)}) copy-start(s32[4]{0:T(128)} %param.15) | copy-start | bytes 52
  66.7 15.0 %all-to-all-start.5 = ((bf16[1,1,4,128,512]{4,3,1,0,2:T(8,128)(2,1)}), bf16[1,1,4,128,512]{4,3,1,0,2:T(8,128)(2,1)S(1)}, u32[]{:S(2)}, u32[]{:S(2)}) async-start(bf16[1,1,4,128,512]{4,3,1,0,2:T(8,128)(2,1)} %bitcast.21), calls=%async_computation.5 | async-start | bytes 1048576 | tf_op jit(solution)/shard_map/all_to_all | solution.py:74
  81.7 15.6 %all-to-all-start.1 = ((bf16[1,1,4,128,512]{4,3,1,0,2:T(8,128)(2,1)}), bf16[1,1,4,128,512]{4,3,1,0,2:T(8,128)(2,1)S(1)}, u32[]{:S(2)}, u32[]{:S(2)}) async-start(bf16[1,1,4,128,512]{4,3,1,0,2:T(8,128)(2,1)} %bitcast.5), calls=%async_computation.1 | async-start | bytes 1048576 | tf_op jit(solution)/shard_map/all_to_all | solution.py:81
  98.7 1.0 copy-start.2
where the time goes:
time: 117 us; the launch traced here: 116 us
  blocking collectives  40.4 us (35%)
  waiting for transfers between devices  40.1 us (34%)
  starting transfers between devices  19.8 us (17%)
  local copies, waits for them, and re-layouts  10.2 us (9%)
  matrix products  2.8 us (2%)
  other arithmetic  2.19 us (2%)
    all_to_all x1, blocking collectives, shards(): lax.all_to_all(attended_heads, 'seq', split_axis=0, concat_axis=1, tiled=...  12.2 us
    all_to_all x1, blocking collectives, shards(): lax.all_to_all(regroup(query_tiles), 'sect', split_axis=1, concat_axis=3,...  10.7 us
    all_to_all x1, waiting for transfers between devices, shards(): lax.all_to_all(lax.all_to_all(regroup(key_tiles), 'sect', split_axis=1, c...  10.7 us
    all_to_all x1, waiting for transfers between devices, shards(): lax.all_to_all(lax.all_to_all(regroup(query_tiles), 'sect', split_axis=1,...  10.1 us
    all_to_all x1, blocking collectives, shards(): lax.all_to_all(regroup(key_tiles), 'sect', split_axis=1, concat_axis=3, t...  9.08 us
    all_to_all x1, waiting for transfers between devices, shards(): lax.all_to_all(lax.all_to_all(regroup(value_tiles), 'sect', split_axis=1,...  8.71 us
    all_to_all x1, blocking collectives, shards(): lax.all_to_all(text_values[0], 'seq', split_axis=1, concat_axis=0, tiled=...  8.41 us
    all_to_all x1, waiting for transfers between devices, shards(): lax.all_to_all(regroup(value_tiles), 'sect', split_axis=1, concat_axis=3,...  5.72 us
  transfers between devices with their start and end apart: 5, of which 5 were waited for; matrix products, arithmetic and copies ran while one was open for 5% of the time, Pallas kernels for 0%

commit v1 on v0

--- a/solution.py
+++ b/solution.py
@@ -1,8 +1,11 @@
+import functools
 import math
 
 import jax
 import jax.numpy as jnp
 from jax import lax
+from jax.experimental import pallas as pl
+from jax.experimental.pallas import tpu as pltpu
 from jax.sharding import PartitionSpec as P
 
 HD = 128
@@ -110,6 +113,195 @@
     return attended[None]
 
 
+def peer_order(sect_count, tile_count):
+    half = tile_count // 2
+    steps = sorted(range(tile_count), key=lambda step: abs(step - half))
+    pairs = [(o, step) for step in steps for o in reversed(range(sect_count))]
+    return [pair for pair in pairs if pair != (0, 0)]
+
+
+def relay_kernel(
+    sizes,
+    q_ref, k_ref, v_ref, tk_ref, tv_ref, len_ref,
+    out_ref,
+    buf, tbuf, obuf,
+    send_sem, recv_sem, text_send, text_recv, out_send, out_recv,
+):
+    sect_count, seq_count, tile_count, heads, part_blocks, rows, text_part = sizes
+    me_s, me_q, me_d = lax.axis_index("sect"), lax.axis_index("seq"), lax.axis_index("dp")
+    mesh_ids = pl.DeviceIdType.MESH
+    width = heads * HD
+    order = peer_order(sect_count, tile_count)
+    block_rows = tile_count * rows
+    text_rows = text_part * seq_count
+
+    def group_peer(offset):
+        return lax.rem(me_s + offset[0], sect_count), lax.rem(me_d + offset[1], tile_count)
+
+    barrier = pltpu.get_barrier_semaphore()
+    for offset in order:
+        to_s, to_d = group_peer(offset)
+        pl.semaphore_signal(barrier, inc=1, device_id={"sect": to_s, "dp": to_d}, device_id_type=mesh_ids)
+    for step in range(1, seq_count):
+        to_q = lax.rem(me_q + step, seq_count)
+        pl.semaphore_signal(barrier, inc=1, device_id={"seq": to_q}, device_id_type=mesh_ids)
+
+    sources = (q_ref, k_ref, v_ref)
+    texts = (tk_ref, tv_ref)
+
+    def piece(number, clip, c):
+        return sources[number].at[clip, :, :, pl.ds(c * HD, HD)]
+
+    def landing(number, c):
+        return buf.at[c, number, pl.ds(me_s * part_blocks, part_blocks), me_d]
+
+    mine = me_s * tile_count + me_d
+    for c in range(heads):
+        for number in range(3):
+            pltpu.make_async_copy(piece(number, mine, c), landing(number, c), recv_sem.at[c]).start()
+    my_text = pl.ds(me_q * text_part, text_part)
+    for number in range(2):
+        pltpu.make_async_copy(
+            texts[number].at[:, pl.ds(pl.multiple_of(me_q * width, HD), width)],
+            tbuf.at[number, my_text],
+            text_recv,
+        ).start()
+
+    pl.semaphore_wait(barrier, len(order) + seq_count - 1)
+
+    def send_chunk(c):
+        for offset in order:
+            to_s, to_d = group_peer(offset)
+            for number in range(3):
+                pltpu.make_async_remote_copy(
+                    src_ref=piece(number, to_s * tile_count + to_d, c),
+                    dst_ref=landing(number, c),
+                    send_sem=send_sem.at[number],
+                    recv_sem=recv_sem.at[c],
+                    device_id={"sect": to_s, "dp": to_d},
+                    device_id_type=mesh_ids,
+                ).start()
+
+    send_chunk(0)
+    for step in range(1, seq_count):
+        to_q = lax.rem(me_q + step, seq_count)
+        for number in range(2):
+            pltpu.make_async_remote_copy(
+                src_ref=texts[number].at[:, pl.ds(pl.multiple_of(to_q * width, HD), width)],
+                dst_ref=tbuf.at[number, my_text],
+                send_sem=text_send,
+                recv_sem=text_recv,
+                device_id={"seq": to_q},
+                device_id_type=mesh_ids,
+            ).start()
+    for c in range(1, heads):
+        send_chunk(c)
+
+    factor = math.log2(math.e) / math.sqrt(HD)
+    pltpu.make_async_copy(tbuf, tbuf, text_recv).wait()
+    live = lax.broadcasted_iota(jnp.int32, (1, text_rows), 1) < len_ref[0]
+    contract_last = (((1,), (1,)), ((), ()))
+    for c in range(heads):
+        pltpu.make_async_copy(buf.at[c], buf.at[c], recv_sem.at[c]).wait()
+        columns = slice(c * HD, (c + 1) * HD)
+        keys = buf[c, 1].reshape(seq_count * block_rows, HD)
+        values = buf[c, 2].reshape(seq_count * block_rows, HD)
+        keys_text = tbuf[0, :, columns]
+        values_text = tbuf[1, :, columns]
+        for step in list(range(1, seq_count)) + [0]:
+            to_q = lax.rem(me_q + step, seq_count)
+            queries = buf[c, 0, to_q].reshape(block_rows, HD)
+            video = lax.dot_general(queries, keys, contract_last, preferred_element_type=jnp.float32)
+            text = lax.dot_general(queries, keys_text, contract_last, preferred_element_type=jnp.float32)
+            text = jnp.where(live, text, -jnp.inf)
+            top = jnp.maximum(jnp.max(video, axis=1, keepdims=True), jnp.max(text, axis=1, keepdims=True))
+            video = jnp.exp2((video - top) * factor)
+            text = jnp.exp2((text - top) * factor)
+            total = jnp.sum(video, axis=1, keepdims=True) + jnp.sum(text, axis=1, keepdims=True)
+            mixed = jnp.dot(video.astype(jnp.bfloat16), values, preferred_element_type=jnp.float32)
+            mixed = mixed + jnp.dot(
+                text.astype(jnp.bfloat16), values_text, preferred_element_type=jnp.float32
+            )
+            obuf[c, step] = (mixed / total).astype(jnp.bfloat16)
+            place = out_ref.at[:, pl.ds(pl.multiple_of((me_q * heads + c) * HD, HD), HD)]
+            if step == 0:
+                pltpu.make_async_copy(obuf.at[c, step], place, out_recv).start()
+            else:
+                pltpu.make_async_remote_copy(
+                    src_ref=obuf.at[c, step],
+                    dst_ref=place,
+                    send_sem=out_send,
+                    recv_sem=out_recv,
+                    device_id={"seq": to_q},
+                    device_id_type=mesh_ids,
+                ).start()
+
+    for number in range(3):
+        view = sources[number].at[pl.ds(0, len(order))]
+        pltpu.make_async_copy(view, view, send_sem.at[number]).wait()
+    text_view = tbuf.at[:, pl.ds(0, text_part * (seq_count - 1))]
+    pltpu.make_async_copy(text_view, text_view, text_send).wait()
+    out_view = obuf.at[:, pl.ds(1, seq_count - 1)]
+    pltpu.make_async_copy(out_view, out_view, out_send).wait()
+    pltpu.make_async_copy(out_ref, out_ref, out_recv).wait()
+
+
+def place_kernel(place_ref, rows_ref, out_ref):
+    out_ref[...] = rows_ref[...]
+
+
+def fused_shards(query_tiles, key_tiles, value_tiles, text_keys, text_values, text_lengths, tile_place):
+    sect_count, seq_count, tile_count = (lax.axis_size(name) for name in ("sect", "seq", "dp"))
+    clips, part_rows, width = query_tiles.shape[1:]
+    rows = part_rows * sect_count // seq_count
+    heads = width // HD
+    part_blocks = part_rows // rows
+    text_part, all_width = text_keys.shape[1:]
+    out_rows = tile_count * rows
+    sizes = (sect_count, seq_count, tile_count, heads, part_blocks, rows, text_part)
+    hbm = pl.BlockSpec(memory_space=pl.ANY)
+
+    def blocks(piece):
+        return piece.reshape(clips, part_blocks, rows, width)
+
+    gathered = pl.pallas_call(
+        functools.partial(relay_kernel, sizes),
+        out_shape=jax.ShapeDtypeStruct((out_rows, all_width), jnp.bfloat16),
+        in_specs=[hbm] * 5 + [pl.BlockSpec(memory_space=pltpu.SMEM)],
+        out_specs=hbm,
+        scratch_shapes=[
+            pltpu.VMEM((heads, 3, seq_count, tile_count, rows, HD), jnp.bfloat16),
+            pltpu.VMEM((2, text_part * seq_count, width), jnp.bfloat16),
+            pltpu.VMEM((heads, seq_count, out_rows, HD), jnp.bfloat16),
+            pltpu.SemaphoreType.DMA((3,)),
+            pltpu.SemaphoreType.DMA((heads,)),
+            pltpu.SemaphoreType.DMA,
+            pltpu.SemaphoreType.DMA,
+            pltpu.SemaphoreType.DMA,
+            pltpu.SemaphoreType.DMA,
+        ],
+        compiler_params=pltpu.CompilerParams(collective_id=0, has_side_effects=True),
+    )(
+        blocks(query_tiles),
+        blocks(key_tiles),
+        blocks(value_tiles),
+        text_keys[0],
+        text_values[0],
+        text_lengths,
+    )
+    attended = pl.pallas_call(
+        place_kernel,
+        grid_spec=pltpu.PrefetchScalarGridSpec(
+            num_scalar_prefetch=1,
+            grid=(tile_count,),
+            in_specs=[pl.BlockSpec((rows, all_width), lambda t, place: (t, 0))],
+            out_specs=pl.BlockSpec((rows, all_width), lambda t, place: (place[t], 0)),
+        ),
+        out_shape=jax.ShapeDtypeStruct((out_rows, all_width), jnp.bfloat16),
+    )(tile_place, gathered)
+    return attended[None]
+
+
 def solution(mesh):
     in_specs = (
         P("dp", None, "sect", "seq"),
@@ -121,4 +313,9 @@
         P(),
     )
     out_specs = P(("sect", "dp"), "seq", None)
-    return jax.shard_map(shards, mesh=mesh, in_specs=in_specs, out_specs=out_specs, check_vma=False)
+
+    def pick(*operands):
+        rows = operands[0].shape[2] * mesh.shape["sect"] // mesh.shape["seq"]
+        return (shards if rows % 16 else fused_shards)(*operands)
+
+    return jax.shard_map(pick, mesh=mesh, in_specs=in_specs, out_specs=out_specs, check_vma=False)

time: 117 us -> 48.2 us (0.41)
  Pallas kernels: 0 us -> 47.3 us
  blocking collectives: 40.4 us -> 0 us
  waiting for transfers between devices: 40.1 us -> 0 us
  starting transfers between devices: 19.8 us -> 0 us
  local copies, waits for them, and re-layouts: 10.2 us -> 0 us
  matrix products: 2.8 us -> 0 us
  other arithmetic: 2.19 us -> 0 us
    pallas_call x0 -> x2, Pallas kernels: none -> 47.3 us  [the longest x1 43.5 us: fused_shards(): pl.pallas_call(functools.partial(relay_kernel, sizes), out_shape=jax.Shap...]
    all_to_all x4 -> x0, blocking collectives: 40.4 us -> none  [the longest x1 12.2 us: shards(): lax.all_to_all(attended_heads, 'seq', split_axis=0, concat_axis=1, tiled=...]
    all_to_all x5 -> x0, waiting for transfers between devices: 40.1 us -> none  [the longest x1 10.7 us: shards(): lax.all_to_all(lax.all_to_all(regroup(key_tiles), 'sect', split_axis=1, c...]
    all_to_all x5 -> x0, starting transfers between devices: 19.8 us -> none  [the longest x1 5.14 us: shards(): lax.all_to_all(lax.all_to_all(regroup(query_tiles), 'sect', split_axis=1,...]
    all_to_all x9 -> x0, local copies, waits for them, and re-layouts: 5.88 us -> none  [the longest x2 1.97 us: shards(): lax.all_to_all(text_keys[0], 'seq', split_axis=1, concat_axis=0, tiled=True)]
    dot_general x4 -> x0, matrix products: 2.8 us -> none  [the longest x1 0.95 us: one_block(): jnp.einsum('hqk,khd->qhd', expo_video.astype(jnp.bfloat16), values_video,...]
    gather x3 -> x0, local copies, waits for them, and re-layouts: 1.74 us -> none  [arrange(): placed = jnp.take(grid, spatial_order, axis=0)]
    reduce_sum x2 -> x0, other arithmetic: 1.21 us -> none  [one_block(): denominators = jnp.sum(expo_video, axis=-1) + jnp.sum(expo_text, axis=-1)]
  transfers between devices with their start and end apart: 5 -> 0, of which waited for: 5 -> 0; matrix products, arithmetic and copies ran while one was open for 5% -> 0% of each run, Pallas kernels for 0% -> 0%
where the time goes in v1:
time: 48.2 us; the launch traced here: 48 us
  Pallas kernels  47.3 us (98%)
  between operations  0.66 us (1%)
    pallas_call x1, Pallas kernels, fused_shards(): pl.pallas_call(functools.partial(relay_kernel, sizes), out_shape=jax.Shap...  43.5 us
    pallas_call x1, Pallas kernels, fused_shards(): pl.pallas_call(place_kernel, grid_spec=pltpu.PrefetchScalarGridSpec(num_s...  3.83 us

profile of v1, /device:TPU:0, one launch (start us, length us, event | category | flops | bytes accessed | tf_op | source)
XLA Modules:
  0.0 48.0 jit_solution(17640622809015722320)
XLA Ops:
  0.7 43.5 %shard_map.73.rows_ref = bf16[128,2048]{1,0:T(8,128)(2,1)} custom-call(bf16[8,2,32,512]{3,2,1,0:T(8,128)(2,1)} %bitcast.6, bf16[8,2,32,512]{3,2,1,0:T(8,128)(2,1)} %bitcast.7, bf16[8,2,32,512]{3,2,1,0:T(8,128)(2,1)} %bitcast.8, bf16[64,2048]{1,0:T(8,128)(2,1)} %bitcast.9, bf16[64,2048]{1,0:T(8,128)(2,1)} %bitcast.10, s32[1]{0:T(128)S(6)} %copy.8.len_ref), custom_call_target="tpu_custom_call" | custom-call | tf_op jit(solution)/shard_map/pallas_call | solution.py:267
  44.2 3.8 %shard_map.74 = bf16[128,2048]{1,0:T(8,128)(2,1)} custom-call(s32[4]{0:T(128)} %place_ref.1, bf16[128,2048]{1,0:T(8,128)(2,1)} %shard_map.73.rows_ref), custom_call_target="tpu_custom_call" | custom-call | tf_op jit(solution)/shard_map/pallas_call | solution.py:292

commit v2 on v1

--- a/solution.py
+++ b/solution.py
@@ -117,15 +117,16 @@
     half = tile_count // 2
     steps = sorted(range(tile_count), key=lambda step: abs(step - half))
     pairs = [(o, step) for step in steps for o in reversed(range(sect_count))]
-    return [pair for pair in pairs if pair != (0, 0)]
+    pairs = [pair for pair in pairs if pair != (0, 0)]
+    return pairs
 
 
 def relay_kernel(
     sizes,
-    q_ref, k_ref, v_ref, tk_ref, tv_ref, len_ref,
+    q_ref, k_ref, v_ref, tk_ref, tv_ref, len_in, place_in,
     out_ref,
-    buf, tbuf, obuf,
-    send_sem, recv_sem, text_send, text_recv, out_send, out_recv,
+    qbufs, kbuf, vbuf, tbuf, pbuf, dbuf, obuf, len_ref, place_ref,
+    send_sem, recv_sem, text_send, text_recv, out_send, out_recv, scalar_sems,
 ):
     sect_count, seq_count, tile_count, heads, part_blocks, rows, text_part = sizes
     me_s, me_q, me_d = lax.axis_index("sect"), lax.axis_index("seq"), lax.axis_index("dp")
@@ -138,6 +139,12 @@
     def group_peer(offset):
         return lax.rem(me_s + offset[0], sect_count), lax.rem(me_d + offset[1], tile_count)
 
+    scalars = (
+        pltpu.make_async_copy(len_in, len_ref, scalar_sems.at[0]),
+        pltpu.make_async_copy(place_in, place_ref, scalar_sems.at[1]),
+    )
+    for copy in scalars:
+        copy.start()
     barrier = pltpu.get_barrier_semaphore()
     for offset in order:
         to_s, to_d = group_peer(offset)
@@ -153,12 +160,16 @@
         return sources[number].at[clip, :, :, pl.ds(c * HD, HD)]
 
     def landing(number, c):
-        return buf.at[c, number, pl.ds(me_s * part_blocks, part_blocks), me_d]
+        blocks = pl.ds(me_s * part_blocks, part_blocks)
+        return (qbufs[c], kbuf.at[c], vbuf.at[c])[number].at[blocks, me_d]
+
+    def arrival(number, c):
+        return recv_sem.at[number, c]
 
     mine = me_s * tile_count + me_d
     for c in range(heads):
         for number in range(3):
-            pltpu.make_async_copy(piece(number, mine, c), landing(number, c), recv_sem.at[c]).start()
+            pltpu.make_async_copy(piece(number, mine, c), landing(number, c), arrival(number, c)).start()
     my_text = pl.ds(me_q * text_part, text_part)
     for number in range(2):
         pltpu.make_async_copy(
@@ -177,7 +188,7 @@
                     src_ref=piece(number, to_s * tile_count + to_d, c),
                     dst_ref=landing(number, c),
                     send_sem=send_sem.at[number],
-                    recv_sem=recv_sem.at[c],
+                    recv_sem=arrival(number, c),
                     device_id={"sect": to_s, "dp": to_d},
                     device_id_type=mesh_ids,
                 ).start()
@@ -199,18 +210,26 @@
 
     factor = math.log2(math.e) / math.sqrt(HD)
     pltpu.make_async_copy(tbuf, tbuf, text_recv).wait()
+    for copy in scalars:
+        copy.wait()
     live = lax.broadcasted_iota(jnp.int32, (1, text_rows), 1) < len_ref[0]
+    holders = []
+    for place in range(tile_count):
+        holder = jnp.int32(0)
+        for slot in range(1, tile_count):
+            holder = jnp.where(place_ref[slot] == place, slot, holder)
+        holders.append(holder)
     contract_last = (((1,), (1,)), ((), ()))
     for c in range(heads):
-        pltpu.make_async_copy(buf.at[c], buf.at[c], recv_sem.at[c]).wait()
+        pltpu.make_async_copy(qbufs[c], qbufs[c], arrival(0, c)).wait()
+        pltpu.make_async_copy(kbuf.at[c], kbuf.at[c], arrival(1, c)).wait()
         columns = slice(c * HD, (c + 1) * HD)
-        keys = buf[c, 1].reshape(seq_count * block_rows, HD)
-        values = buf[c, 2].reshape(seq_count * block_rows, HD)
+        keys = kbuf[c].reshape(seq_count * block_rows, HD)
         keys_text = tbuf[0, :, columns]
-        values_text = tbuf[1, :, columns]
-        for step in list(range(1, seq_count)) + [0]:
+        steps = list(range(1, seq_count)) + [0]
+        for step in steps:
             to_q = lax.rem(me_q + step, seq_count)
-            queries = buf[c, 0, to_q].reshape(block_rows, HD)
+            queries = jnp.concatenate([qbufs[c][to_q, slot] for slot in holders], axis=0)
             video = lax.dot_general(queries, keys, contract_last, preferred_element_type=jnp.float32)
             text = lax.dot_general(queries, keys_text, contract_last, preferred_element_type=jnp.float32)
             text = jnp.where(live, text, -jnp.inf)
@@ -218,11 +237,17 @@
             video = jnp.exp2((video - top) * factor)
             text = jnp.exp2((text - top) * factor)
             total = jnp.sum(video, axis=1, keepdims=True) + jnp.sum(text, axis=1, keepdims=True)
-            mixed = jnp.dot(video.astype(jnp.bfloat16), values, preferred_element_type=jnp.float32)
-            mixed = mixed + jnp.dot(
-                text.astype(jnp.bfloat16), values_text, preferred_element_type=jnp.float32
-            )
-            obuf[c, step] = (mixed / total).astype(jnp.bfloat16)
+            pbuf[step, :, : video.shape[1]] = video.astype(jnp.bfloat16)
+            pbuf[step, :, video.shape[1] :] = text.astype(jnp.bfloat16)
+            dbuf[step] = jnp.broadcast_to(total, (block_rows, HD))
+        pltpu.make_async_copy(vbuf.at[c], vbuf.at[c], arrival(2, c)).wait()
+        values = jnp.concatenate(
+            [vbuf[c].reshape(seq_count * block_rows, HD), tbuf[1, :, columns]], axis=0
+        )
+        for step in steps:
+            to_q = lax.rem(me_q + step, seq_count)
+            mixed = jnp.dot(pbuf[step], values, preferred_element_type=jnp.float32)
+            obuf[c, step] = (mixed / dbuf[step]).astype(jnp.bfloat16)
             place = out_ref.at[:, pl.ds(pl.multiple_of((me_q * heads + c) * HD, HD), HD)]
             if step == 0:
                 pltpu.make_async_copy(obuf.at[c, step], place, out_recv).start()
@@ -246,10 +271,6 @@
     pltpu.make_async_copy(out_ref, out_ref, out_recv).wait()
 
 
-def place_kernel(place_ref, rows_ref, out_ref):
-    out_ref[...] = rows_ref[...]
-
-
 def fused_shards(query_tiles, key_tiles, value_tiles, text_keys, text_values, text_lengths, tile_place):
     sect_count, seq_count, tile_count = (lax.axis_size(name) for name in ("sect", "seq", "dp"))
     clips, part_rows, width = query_tiles.shape[1:]
@@ -266,19 +287,26 @@
 
     gathered = pl.pallas_call(
         functools.partial(relay_kernel, sizes),
-        out_shape=jax.ShapeDtypeStruct((out_rows, all_width), jnp.bfloat16),
-        in_specs=[hbm] * 5 + [pl.BlockSpec(memory_space=pltpu.SMEM)],
-        out_specs=hbm,
+        out_shape=pltpu.VMEM((out_rows, all_width), jnp.bfloat16),
+        in_specs=[hbm] * 7,
+        out_specs=pl.BlockSpec(memory_space=pltpu.VMEM),
         scratch_shapes=[
-            pltpu.VMEM((heads, 3, seq_count, tile_count, rows, HD), jnp.bfloat16),
+            [pltpu.VMEM((seq_count, tile_count, rows, HD), jnp.bfloat16)] * heads,
+            pltpu.VMEM((heads, seq_count, tile_count, rows, HD), jnp.bfloat16),
+            pltpu.VMEM((heads, seq_count, tile_count, rows, HD), jnp.bfloat16),
             pltpu.VMEM((2, text_part * seq_count, width), jnp.bfloat16),
+            pltpu.VMEM((seq_count, out_rows, seq_count * (out_rows + text_part)), jnp.bfloat16),
+            pltpu.VMEM((seq_count, out_rows, HD), jnp.float32),
             pltpu.VMEM((heads, seq_count, out_rows, HD), jnp.bfloat16),
+            pltpu.SMEM((1,), jnp.int32),
+            pltpu.SMEM((tile_count,), jnp.int32),
             pltpu.SemaphoreType.DMA((3,)),
-            pltpu.SemaphoreType.DMA((heads,)),
+            pltpu.SemaphoreType.DMA((3, heads)),
             pltpu.SemaphoreType.DMA,
             pltpu.SemaphoreType.DMA,
             pltpu.SemaphoreType.DMA,
             pltpu.SemaphoreType.DMA,
+            pltpu.SemaphoreType.DMA((2,)),
         ],
         compiler_params=pltpu.CompilerParams(collective_id=0, has_side_effects=True),
     )(
@@ -288,18 +316,9 @@
         text_keys[0],
         text_values[0],
         text_lengths,
-    )
-    attended = pl.pallas_call(
-        place_kernel,
-        grid_spec=pltpu.PrefetchScalarGridSpec(
-            num_scalar_prefetch=1,
-            grid=(tile_count,),
-            in_specs=[pl.BlockSpec((rows, all_width), lambda t, place: (t, 0))],
-            out_specs=pl.BlockSpec((rows, all_width), lambda t, place: (place[t], 0)),
-        ),
-        out_shape=jax.ShapeDtypeStruct((out_rows, all_width), jnp.bfloat16),
-    )(tile_place, gathered)
-    return attended[None]
+        tile_place,
+    )
+    return gathered[None]
 
 
 def solution(mesh):

time: 48.2 us -> 44.7 us (0.927)
  Pallas kernels: 47.3 us -> 43.1 us
  local copies, waits for them, and re-layouts: 0 us -> 0.8 us
    pallas_call x2 -> x1, Pallas kernels: 47.3 us -> 43.1 us  [fused_shards(): pl.pallas_call(functools.partial(relay_kernel, sizes), out_shape=pltpu.VM...]
    unnamed x0 -> x1, local copies, waits for them, and re-layouts: none -> 0.8 us
where the time goes in v2:
time: 44.7 us; the launch traced here: 44.5 us
  Pallas kernels  43.1 us (96%)
  local copies, waits for them, and re-layouts  0.8 us (2%)
  between operations  0.66 us (1%)
    pallas_call x1, Pallas kernels, fused_shards(): pl.pallas_call(functools.partial(relay_kernel, sizes), out_shape=pltpu.VM...  43.1 us

profile of v2, /device:TPU:0, one launch (start us, length us, event | category | flops | bytes accessed | tf_op | source)
XLA Modules:
  0.0 44.5 jit_solution(2028975845251160980)
XLA Ops:
  0.7 43.1 %shard_map.73 = bf16[128,2048]{1,0:T(8,128)(2,1)S(1)} custom-call(bf16[8,2,32,512]{3,2,1,0:T(8,128)(2,1)} %bitcast.7, bf16[8,2,32,512]{3,2,1,0:T(8,128)(2,1)} %bitcast.8, bf16[8,2,32,512]{3,2,1,0:T(8,128)(2,1)} %bitcast.9, bf16[64,2048]{1,0:T(8,128)(2,1)} %bitcast.10, bf16[64,2048]{1,0:T(8,128)(2,1)} %bitcast.11, s32[1]{0:T(128)S(6)} %copy.10.len_in, s32[4]{0:T(128)} %place_in.1), custom_call_target="tpu_custom_call" | custom-call | tf_op jit(solution)/shard_map/pallas_call | solution.py:288
  43.7 0.8 %copy.9 = bf16[1,128,2048]{2,1,0:T(8,128)(2,1)} copy(bf16[1,128,2048]{2,1,0:T(8,128)(2,1)S(1)} %bitcast.6) | data formatting | bytes 1048576
